TPU v7x, 256 devices: a whole 4x4x8 slice. The times are simulated.
256 devices in a mesh: row: 32 (over y, z), col: 8 (over x, core).
Axes of the slice: x: 4, y: 4, z: 8, core: 2. Of those that a mesh axis runs over, the one named last changes fastest.
Arguments:
- load_currents: float32 [16, 256, 128, 128], P(None, 'row', 'col'), may hold values from -24 to 24
- block_library: float32 [8, 128, 128], replicated, may hold values from -4.0625 to 24.1, as said below
- strap_conductance: float32 [2, 128], replicated, may hold values from 0.5 to 4
- block_types: int32 [256, 128], P('row', 'col'), may hold values from 0 to 7
- aggregate_map: int32 [256, 128], P('row', 'col'), may hold values from 0 to 255, as said below
Outputs:
- node_voltage: float32 [16, 256, 128, 128], P(None, 'row', 'col')
- residual: float32 [16, 256, 128, 128], P(None, 'row', 'col')
Inputs may be any that keep to these rules, and one draw needn't show every extreme that they name: `aggregate_map`: each aggregate id names an aggregate of one column group of 16 block columns; the same id in another column group is another aggregate. Every aggregate of every column group holds at least one block. `block_library`: each library block is symmetric positive definite, with nonpositive off-diagonal entries and positive row sums.
All inputs are finite; a program needn't handle non-finite values.
Results may differ from a plain program's by a relative error of at most 0.0003.
Values sent between devices are 32-bit elements; how exact they have to be, the bound alone decides.
A program may use at most 64 MiB of HBM per device.

v0:
```python
import jax
import jax.numpy as jnp
from jax import lax
from jax.sharding import PartitionSpec as P

SWEEPS = 3
ITERS = 2
AGR = 4
AGC = 4


def padded_2(array, sides, width):
    for axis, dim in sides:
        size, length = (lax.axis_size(axis), array.shape[dim])
        up = [(i, (i + 1) % size) for i in range(size - 1)]
        down = [(j, i) for i, j in up]
        last = lax.slice_in_dim(array, length - width, length, axis=dim)
        first = lax.slice_in_dim(array, 0, width, axis=dim)
        before = lax.ppermute(last, axis, up)
        after = lax.ppermute(first, axis, down)
        array = jnp.concatenate([before, array, after], axis=dim)
    return array


def from_behind(array, axis, by):
    length = lax.axis_size(axis)
    pairs = [(i, i + by) for i in range(length) if 0 <= i + by < length]
    return lax.ppermute(array, axis, pairs)


def coarse_terms(group_ids, group_types, block_sums, north_weight, east_weight, count):
    centre = block_sums[group_types] + 2.0 * north_weight + 2.0 * east_weight
    flat = group_ids.reshape(-1)
    upper = group_ids[:-1].reshape(-1)
    lower = group_ids[1:].reshape(-1)
    left = group_ids[:, :-1].reshape(-1)
    right = group_ids[:, 1:].reshape(-1)
    index = jnp.concatenate(
        [
            flat * count + flat,
            upper * count + lower,
            lower * count + upper,
            left * count + right,
            right * count + left,
        ]
    )
    values = jnp.concatenate(
        [
            centre.reshape(-1),
            -north_weight * jnp.ones((2 * upper.shape[0],), jnp.float32),
            -east_weight * jnp.ones((2 * left.shape[0],), jnp.float32),
        ]
    )
    return jax.ops.segment_sum(values, index, num_segments=count * count).reshape(count, count)


def alignment_sum(residual, zeta):
    return lax.psum(jnp.sum(residual * zeta, axis=(1, 2, 3)), ("row", "col"))


def on_device(load_currents, block_library, strap_conductance, block_types, aggregate_map):
    sizings, rows_local, cols_local, nodes = load_currents.shape
    blocks = rows_local * cols_local
    count = rows_local * lax.axis_size("row") // AGR * (cols_local // AGC)
    picked = block_library[block_types.reshape(-1)]
    couple = 2.0 * strap_conductance[0] + 2.0 * strap_conductance[1]
    diag_library = jnp.diagonal(block_library, axis1=1, axis2=2)
    diagonal = diag_library[block_types] + couple
    block_sums = jnp.sum(block_library, axis=(1, 2))
    north_weight = jnp.sum(strap_conductance[0])
    east_weight = jnp.sum(strap_conductance[1])

    def block_products(field):
        flat = field.reshape(sizings, blocks, nodes)
        product = jnp.einsum("bij,sbj->sbi", picked, flat, precision=lax.Precision.HIGHEST)
        return product.reshape(sizings, rows_local, cols_local, nodes)

    local_matrix = coarse_terms(
        aggregate_map, block_types, block_sums, north_weight, east_weight, count
    )
    below_ids = from_behind(aggregate_map[0], "row", -1)
    present = (lax.axis_index("row") < lax.axis_size("row") - 1).astype(jnp.float32)
    bottom_ids = aggregate_map[-1]
    cross_index = jnp.concatenate([bottom_ids * count + below_ids, below_ids * count + bottom_ids])
    cross_values = -north_weight * present * jnp.ones((2 * cols_local,), jnp.float32)
    cross_matrix = jax.ops.segment_sum(
        cross_values, cross_index, num_segments=count * count
    ).reshape(count, count)
    coarse_matrix = lax.psum(local_matrix + cross_matrix, "row")
    factor = jnp.linalg.cholesky(coarse_matrix)
    flat_ids = aggregate_map.reshape(-1)

    def smooth(residual):
        result = residual / diagonal
        for sweep in range(SWEEPS - 1):
            image = block_products(result) + couple * result
            result = result + (residual - image) / diagonal
        return result

    def coarse_part(residual):
        sums = residual.sum(-1).reshape(sizings, blocks).T
        local = jax.ops.segment_sum(sums, flat_ids, num_segments=count)
        gathered = lax.psum(local, "row")
        solved = jax.scipy.linalg.cho_solve((factor, True), gathered)
        return solved[flat_ids].T.reshape(sizings, rows_local, cols_local)[..., None]

    def precondition(residual):
        return smooth(residual) + coarse_part(residual)

    node_voltage = jnp.zeros_like(load_currents)
    residual = load_currents
    zeta = precondition(residual)
    direction = zeta
    aligned = alignment_sum(residual, zeta)
    for iteration in range(ITERS):
        padded = padded_2(direction, (("row", 1), ("col", 2)), 1)
        north = padded[:, :-2, 1:-1]
        south = padded[:, 2:, 1:-1]
        west = padded[:, 1:-1, :-2]
        east = padded[:, 1:-1, 2:]
        lateral = strap_conductance[0] * (2.0 * direction - north - south) + strap_conductance[
            1
        ] * (2.0 * direction - west - east)
        image = block_products(direction) + lateral
        curvature = lax.psum(jnp.sum(direction * image, axis=(1, 2, 3)), ("row", "col"))
        step_size = (aligned / curvature)[:, None, None, None]
        node_voltage = node_voltage + step_size * direction
        residual = residual - step_size * image
        if iteration + 1 < ITERS:
            zeta = precondition(residual)
            fresh = alignment_sum(residual, zeta)
            blend = (fresh / aligned)[:, None, None, None]
            direction = zeta + blend * direction
            aligned = fresh
    return (node_voltage, residual)


def solution(mesh):
    placed = (P(None, "row", "col", None), P(), P(), P("row", "col"), P("row", "col"))
    return jax.shard_map(
        on_device,
        mesh=mesh,
        in_specs=placed,
        out_specs=(P(None, "row", "col", None), P(None, "row", "col", None)),
        check_vma=False,
    )
```

profile of v0, /device:TPU:1, one launch (start us, length us, event | category | flops | bytes accessed | tf_op | source)
XLA Modules:
  0.0 772.2 jit_solution(3687097905419126397)
XLA Ops:
  18.7 5.9 copy.47
  28.8 4.3 gather_fusion.2
  33.8 16.3 %fusion.50 = f32[128,16,128]{2,1,0:T(8,128)S(1)} fusion(f32[16,128,128]{2,0,1:T(8,128)S(1)} %bitcast.139, f32[128,128,128]{2,1,0:T(8,128)} %gather_fusion.2), kind=kOutput, calls=%fused_computation.144 | convolution fusion | flops 402653184 | bytes 10485760 | tf_op jit(solution)/shard_map/bij,sbj->sbi/dot_general | solution.py:75
  50.8 14.2 %fusion.51 = f32[128,16,128]{2,1,0:T(8,128)} fusion(f32[16,128,128]{2,0,1:T(8,128)S(1)} %bitcast.140, f32[128,128,128]{2,1,0:T(8,128)S(1)} %bitcast.127), kind=kOutput, calls=%fused_computation.145 | convolution fusion | flops 402653184 | bytes 10485760 | tf_op jit(solution)/shard_map/bij,sbj->sbi/dot_general | solution.py:75
  66.2 4.7 scatter_custom_fusion
  74.0 120.5 %psum.50 = f32[256,16]{0,1:T(8,128)S(1)} all-reduce(f32[256,16]{0,1:T(8,128)S(1)} %copy.55), channel_id=1, replica_groups=mesh['row'=32,'col'=8] {'row'}, use_global_device_ids=true, to_apply=%region_11.12 | all-reduce | flops 4096 | bytes 32768 | tf_op jit(solution)/shard_map/psum | solution.py:103
  194.5 23.7 %all-reduce.5.cloned.1.call-done = f32[256,256]{0,1:T(8,128)} async-done(((f32[256,256]{0,1:T(8,128)}), f32[256,256]{0,1:T(8,128)}) %all-reduce.5.cloned.1.call-update) | async-done | bytes 262160 | tf_op jit(solution)/shard_map/psum | solution.py:89
  220.3 11.7 %cholesky.50 = f32[128,128]{1,0:T(8,128)S(1)} custom-call(f32[128,128]{1,0:T(8,128)S(1)} %cholesky.118), custom_call_target="Cholesky" | custom-call | tf_op jit(solution)/shard_map/jit(cholesky)/cholesky | solution.py:90
  232.1 9.8 %custom-call.16 = f32[1,128,128]{1,2,0:T(8,128)S(1)} custom-call(f32[1,128,128]{2,1,0:T(8,128)S(1)} %get-tuple-element.55), custom_call_target="InvertDiagBlocksLowerTriangular" | custom-call | tf_op jit(solution)/shard_map/jit(cholesky)/cholesky | solution.py:90
  242.4 11.7 %cholesky.105 = f32[128,128]{1,0:T(8,128)S(1)} custom-call(f32[128,128]{1,0:T(8,128)S(1)} %convolution_subtract_fusion), custom_call_target="Cholesky" | custom-call | tf_op jit(solution)/shard_map/jit(cholesky)/cholesky | solution.py:90
  256.1 3.8 while.4
  260.0 19.8 %custom-call.20 = f32[2,128,128]{1,2,0:T(8,128)S(1)} custom-call(f32[2,128,128]{2,1,0:T(8,128)S(1)} %get-tuple-element.17), custom_call_target="InvertDiagBlocksLowerTriangular" | custom-call | tf_op jit(solution)/shard_map/jit(_cho_solve)/triangular_solve | solution.py:104
  287.6 4.0 collective-permute-done.2
  291.6 9.7 %collective-permute-start.3 = (f32[16,10,1,128]{3,0,2,1:T(8,128)S(1)}, f32[16,10,1,128]{3,0,2,1:T(8,128)S(1)}, u32[]{:S(2)}, u32[]{:S(2)}) collective-permute-start(f32[16,10,1,128]{3,0,2,1:T(8,128)S(1)} %get-tuple-element.44), channel_id=1, source_target_pairs={{0,1},{1,2},{2,3},{3,4},{4,5},{5,6},{6,7},{8,9},{9,10},{10,11},{11... | collective-permute-start | bytes 245768 | tf_op jit(solution)/shard_map/ppermute | solution.py:19
  303.3 15.4 %fusion.52 = f32[128,16,128]{2,1,0:T(8,128)S(1)} fusion(f32[16,128,128]{2,0,1:T(8,128)S(1)} %bitcast.130, f32[128,128,128]{2,1,0:T(8,128)} %gather_fusion.2), kind=kOutput, calls=%fused_computation.146 | convolution fusion | flops 402653184 | bytes 10485760 | tf_op jit(solution)/shard_map/bij,sbj->sbi/dot_general | solution.py:75
  320.5 77.0 %all-reduce.2 = (f32[16]{0:T(128)S(1)}, f32[16]{0:T(128)S(1)}) all-reduce(f32[16]{0:T(128)S(1)} %get-tuple-element.22, f32[16]{0:T(128)S(1)} %get-tuple-element.21), channel_id=1, replica_groups=mesh['row'=32,'col'=8] {'row','col'}, use_global_device_ids=true, to_apply=%region_13.15 | all-reduce | flops 32 | bytes 256 | tf_op jit(solution)/shard_map/psum | solution.py:58
  399.7 15.8 %divide_add_fusion = (f32[16,8,16,128]{3,0,2,1:T(8,128)S(1)}, f32[16,8,16]{0,2,1:T(8,128)S(1)}, f32[128,16,128]{2,1,0:T(8,128)S(1)}) fusion(f32[16,8,16,128]{3,0,2,1:T(8,128)S(1)} %get-tuple-element.38, f32[128]{0:T(128)S(1)} %add_multiply_fusion, f32[8,16,128]{2,1,0:T(8,128)S(1)} %broadcast_add_fusion, f32[16,128,128]{2,0,1:T(8,128)S(1)} %bitcast.137, ...), kind=kOutput, calls=%fused_computation.54 | convolution fusion | flops 404486144 | bytes 12657152 | tf_op jit(solution)/shard_map/bij,sbj->sbi/dot_general | solution.py:75
  415.5 14.0 %fusion.53 = f32[128,16,128]{2,1,0:T(8,128)} fusion(f32[16,128,128]{2,0,1:T(8,128)S(1)} %bitcast.138, f32[128,128,128]{2,1,0:T(8,128)S(1)} %bitcast.129), kind=kOutput, calls=%fused_computation.147 | convolution fusion | flops 402653184 | bytes 10485760 | tf_op jit(solution)/shard_map/bij,sbj->sbi/dot_general | solution.py:75
  432.4 110.3 %psum.53 = f32[256,16]{0,1:T(8,128)S(1)} all-reduce(f32[256,16]{0,1:T(8,128)S(1)} %copy.61), channel_id=1, replica_groups=mesh['row'=32,'col'=8] {'row'}, use_global_device_ids=true, to_apply=%region_18.20 | all-reduce | flops 4096 | bytes 32768 | tf_op jit(solution)/shard_map/psum | solution.py:103
  549.9 100.2 %psum.54 = f32[16]{0:T(128)S(1)} all-reduce(f32[16]{0:T(128)S(1)} %multiply_reduce_fusion.1), channel_id=1, replica_groups=mesh['row'=32,'col'=8] {'row','col'}, use_global_device_ids=true, to_apply=%region_20.22 | all-reduce | flops 16 | bytes 128 | tf_op jit(solution)/shard_map/psum | solution.py:58
  652.8 3.7 collective-permute-start.5
  662.3 4.3 collective-permute-start.7
  668.5 15.4 %fusion.54 = f32[128,16,128]{2,1,0:T(8,128)S(1)} fusion(f32[16,128,128]{2,0,1:T(8,128)S(1)} %bitcast.131, f32[128,128,128]{2,1,0:T(8,128)} %gather_fusion.2), kind=kOutput, calls=%fused_computation.148 | convolution fusion | flops 402653184 | bytes 10485760 | tf_op jit(solution)/shard_map/bij,sbj->sbi/dot_general | solution.py:75
  685.3 75.4 %psum.55 = f32[16]{0:T(128)S(1)} all-reduce(f32[16]{0:T(128)S(1)} %get-tuple-element.35), channel_id=1, replica_groups=mesh['row'=32,'col'=8] {'row','col'}, use_global_device_ids=true, to_apply=%region_22.24 | all-reduce | flops 16 | bytes 128 | tf_op jit(solution)/shard_map/psum | solution.py:125
  (143 shorter events, 65.4 us)
Async XLA Ops:
  7.2 17.4 %copy-start = (f32[8,128,128]{2,1,0:T(8,128)S(1)}, f32[8,128,128]{2,1,0:T(8,128)}, u32[]{:S(2)}) copy-start(f32[8,128,128]{2,1,0:T(8,128)} %param.8) | copy-start | bytes 1572868
  7.2 211.1 %all-reduce.5.cloned.1.call-start = ((), (), s32[]{:S(2)}) async-start(), calls=%async_computation | async-start | bytes 524288 | tf_op jit(solution)/shard_map/psum | solution.py:89
  8.0 57.3 %collective-permute-start = (s32[16]{0:T(128)S(1)}, s32[16]{0:T(128)S(1)}, u32[]{:S(2)}, u32[]{:S(2)}) collective-permute-start(s32[16]{0:T(128)S(1)} %slice_bitcast_fusion.10), channel_id=1, source_target_pairs={{8,0},{16,8},{24,16},{32,24},{40,32},{48,40},{56,48},{64,56},{72,6... | collective-permute-start | bytes 200 | tf_op jit(solution)/shard_map/ppermute | solution.py:28
  15.6 56.7 %copy-start.6 = (s32[128]{0:T(128)}, s32[128]{0:T(128)S(1)}, u32[]{:S(2)}) copy-start(s32[128]{0:T(128)S(1)} %reshape.186) | copy-start | bytes 1540
  28.8 4.3 copy-start.1
  33.1 17.7 %slice-start = ((s8[8388608]{0:T(1024)(128)(4,1)}), s8[4194304]{0:T(1024)(128)(4,1)S(1)}, s32[]{:S(2)}) async-start(s8[8388608]{0:T(1024)(128)(4,1)} %bitcast.126), calls=%async_computation.1 | async-start | bytes 8388608
  33.8 17.1 %slice-start.1 = ((s8[8388608]{0:T(1024)(128)(4,1)}), s8[4194304]{0:T(1024)(128)(4,1)S(1)}, s32[]{:S(2)}) async-start(s8[8388608]{0:T(1024)(128)(4,1)} %bitcast.126), calls=%async_computation.2 | async-start | bytes 8388608
  279.8 1.2 copy-start.3
  283.8 3.8 collective-permute-start.1
  285.7 5.9 collective-permute-start.2
  291.6 27.0 %collective-permute-start.3 = (f32[16,10,1,128]{3,0,2,1:T(8,128)S(1)}, f32[16,10,1,128]{3,0,2,1:T(8,128)S(1)}, u32[]{:S(2)}, u32[]{:S(2)}) collective-permute-start(f32[16,10,1,128]{3,0,2,1:T(8,128)S(1)} %get-tuple-element.44), channel_id=1, source_target_pairs={{0,1},{1,2},{2,3},{3,4},{4,5},{5,6},{6,7},{8,9},{9,10},{10,11},{11... | collective-permute-start | bytes 245768 | tf_op jit(solution)/shard_map/ppermute | solution.py:19
  301.4 17.3 %collective-permute-start.4 = (f32[16,10,1,128]{3,0,2,1:T(8,128)S(1)}, f32[16,10,1,128]{3,0,2,1:T(8,128)S(1)}, u32[]{:S(2)}, u32[]{:S(2)}) collective-permute-start(f32[16,10,1,128]{3,0,2,1:T(8,128)S(1)} %get-tuple-element.45), channel_id=1, source_target_pairs={{1,0},{2,1},{3,2},{4,3},{5,4},{6,5},{7,6},{9,8},{10,9},{11,10},{12... | collective-permute-start | bytes 245768 | tf_op jit(solution)/shard_map/ppermute | solution.py:20
  397.6 2.1 copy-start.7
  397.6 2.1 copy-start.4
  397.6 17.9 %slice-start.2 = ((s8[8388608]{0:T(1024)(128)(4,1)}), s8[4194304]{0:T(1024)(128)(4,1)S(1)}, s32[]{:S(2)}) async-start(s8[8388608]{0:T(1024)(128)(4,1)} %bitcast.128), calls=%async_computation.3 | async-start | bytes 8388608
  399.7 15.8 %slice-start.3 = ((s8[8388608]{0:T(1024)(128)(4,1)}), s8[4194304]{0:T(1024)(128)(4,1)S(1)}, s32[]{:S(2)}) async-start(s8[8388608]{0:T(1024)(128)(4,1)} %bitcast.128), calls=%async_computation.4 | async-start | bytes 8388608
  415.5 234.6 %copy-start.2 = (f32[128,16,128]{2,1,0:T(8,128)}, f32[128,16,128]{2,1,0:T(8,128)S(1)}, u32[]{:S(2)}) copy-start(f32[128,16,128]{2,1,0:T(8,128)S(1)} %get-tuple-element.72) | copy-start | bytes 3145732
  652.8 108.0 %copy-start.5 = (f32[16]{0:T(128)S(1)}, f32[16]{0:T(128)}, u32[]{:S(2)}) copy-start(f32[16]{0:T(128)} %copy-done.4) | copy-start | bytes 196
  652.8 5.8 collective-permute-start.5
  656.5 5.7 collective-permute-start.6
  662.3 21.6 %collective-permute-start.7 = (f32[16,10,1,128]{3,0,2,1:T(8,128)S(1)}, f32[16,10,1,128]{3,0,2,1:T(8,128)S(1)}, u32[]{:S(2)}, u32[]{:S(2)}) collective-permute-start(f32[16,10,1,128]{3,0,2,1:T(8,128)S(1)} %get-tuple-element.42), channel_id=1, source_target_pairs={{0,1},{1,2},{2,3},{3,4},{4,5},{5,6},{6,7},{8,9},{9,10},{10,11},{11... | collective-permute-start | bytes 245768 | tf_op jit(solution)/shard_map/ppermute | solution.py:19
  666.5 17.3 %collective-permute-start.8 = (f32[16,10,1,128]{3,0,2,1:T(8,128)S(1)}, f32[16,10,1,128]{3,0,2,1:T(8,128)S(1)}, u32[]{:S(2)}, u32[]{:S(2)}) collective-permute-start(f32[16,10,1,128]{3,0,2,1:T(8,128)S(1)} %get-tuple-element.43), channel_id=1, source_target_pairs={{1,0},{2,1},{3,2},{4,3},{5,4},{6,5},{7,6},{9,8},{10,9},{11,10},{12... | collective-permute-start | bytes 245768 | tf_op jit(solution)/shard_map/ppermute | solution.py:20
Sparse Core Ops, SparseCore 0:
  72.0 146.2 all-reduce.4
where the time goes:
time: 779 us; the launch traced here: 772 us
  blocking collectives  483 us (62%)
  matrix products  97.2 us (12%)
  other arithmetic  82.4 us (11%)
  waiting for transfers between devices  32.8 us (4%)
  local copies, waits for them, and re-layouts  30.2 us (4%)
  starting transfers between devices  27.3 us (4%)
  between operations  18.8 us (2%)
    psum x2, blocking collectives, coarse_part(): gathered = lax.psum(local, 'row')  231 us
    psum x2, blocking collectives, alignment_sum(): return lax.psum(jnp.sum(residual * zeta, axis=(1, 2, 3)), ('row', 'col'))  177 us
    dot_general x6, matrix products, block_products(): jnp.einsum('bij,sbj->sbi', picked, flat, precision=lax.Precision.HIGHEST)  91.1 us
    psum x1, blocking collectives, on_device(): lax.psum(jnp.sum(direction * image, axis=(1, 2, 3)), ('row', 'col'))  75.4 us
    another operation x6, other arithmetic, on_device(): factor = jnp.linalg.cholesky(coarse_matrix)  33.9 us
    psum x1, waiting for transfers between devices, on_device(): coarse_matrix = lax.psum(local_matrix + cross_matrix, 'row')  23.7 us
    another operation x6, other arithmetic, coarse_part(): solved = jax.scipy.linalg.cho_solve((factor, True), gathered)  19.9 us
    ppermute x4, starting transfers between devices, padded_2(): before = lax.ppermute(last, axis, up)  19.5 us
  transfers between devices with their start and end apart: 10, of which 5 were waited for; matrix products, arithmetic and copies ran while one was open for 11% of the time, Pallas kernels for 0%

commit v1 on v0

--- a/solution.py
+++ b/solution.py
@@ -100,7 +100,11 @@
     def coarse_part(residual):
         sums = residual.sum(-1).reshape(sizings, blocks).T
         local = jax.ops.segment_sum(sums, flat_ids, num_segments=count)
-        gathered = lax.psum(local, "row")
+        gathered = local
+        for hop in (1, 2, 4, 8, 16):
+            gathered = gathered + lax.ppermute(
+                gathered, "row", [(dev, dev ^ hop) for dev in range(32)]
+            )
         solved = jax.scipy.linalg.cho_solve((factor, True), gathered)
         return solved[flat_ids].T.reshape(sizings, rows_local, cols_local)[..., None]
 

time: 779 us -> 668 us (0.86)
  blocking collectives: 483 us -> 229 us
  waiting for transfers between devices: 32.8 us -> 155 us
  starting transfers between devices: 27.3 us -> 47.7 us
    psum x2 -> x0, blocking collectives: 231 us -> none  [coarse_part(): gathered = lax.psum(local, 'row')]
    psum x1, waiting for transfers between devices: 23.7 us -> 129 us  [on_device(): coarse_matrix = lax.psum(local_matrix + cross_matrix, 'row')]
    psum x2, blocking collectives: 177 us -> 154 us  [alignment_sum(): return lax.psum(jnp.sum(residual * zeta, axis=(1, 2, 3)), ('row', 'col'))]
    ppermute x0 -> x10, starting transfers between devices: none -> 20.2 us  [coarse_part(): lax.ppermute(gathered, 'row', [(dev, dev ^ hop) for dev in range(32)])]
    ppermute x0 -> x10, waiting for transfers between devices: none -> 17.1 us  [coarse_part(): lax.ppermute(gathered, 'row', [(dev, dev ^ hop) for dev in range(32)])]
  transfers between devices with their start and end apart: 10 -> 20, of which waited for: 5 -> 12; matrix products, arithmetic and copies ran while one was open for 11% -> 17% of each run, Pallas kernels for 0% -> 0%
where the time goes in v1:
time: 668 us; the launch traced here: 661 us
  blocking collectives  229 us (34%)
  waiting for transfers between devices  155 us (23%)
  matrix products  97.1 us (15%)
  other arithmetic  83.2 us (12%)
  starting transfers between devices  47.7 us (7%)
  local copies, waits for them, and re-layouts  29.6 us (4%)
  between operations  18.9 us (3%)
    psum x2, blocking collectives, alignment_sum(): return lax.psum(jnp.sum(residual * zeta, axis=(1, 2, 3)), ('row', 'col'))  154 us
    psum x1, waiting for transfers between devices, on_device(): coarse_matrix = lax.psum(local_matrix + cross_matrix, 'row')  129 us
    dot_general x6, matrix products, block_products(): jnp.einsum('bij,sbj->sbi', picked, flat, precision=lax.Precision.HIGHEST)  94.4 us
    psum x1, blocking collectives, on_device(): lax.psum(jnp.sum(direction * image, axis=(1, 2, 3)), ('row', 'col'))  75.3 us
    another operation x6, other arithmetic, on_device(): factor = jnp.linalg.cholesky(coarse_matrix)  33.9 us
    ppermute x10, starting transfers between devices, coarse_part(): lax.ppermute(gathered, 'row', [(dev, dev ^ hop) for dev in range(32)])  20.2 us
    another operation x6, other arithmetic, coarse_part(): solved = jax.scipy.linalg.cho_solve((factor, True), gathered)  19.7 us
    ppermute x4, starting transfers between devices, padded_2(): before = lax.ppermute(last, axis, up)  19.7 us
  transfers between devices with their start and end apart: 20, of which 12 were waited for; matrix products, arithmetic and copies ran while one was open for 17% of the time, Pallas kernels for 0%

profile of v1, /device:TPU:1, one launch (start us, length us, event | category | flops | bytes accessed | tf_op | source)
XLA Modules:
  0.0 660.6 jit_solution(8724587739423088816)
XLA Ops:
  24.5 5.9 copy.47
  35.3 4.3 gather_fusion.2
  39.6 16.3 %fusion.52 = f32[128,16,128]{2,1,0:T(8,128)S(1)} fusion(f32[16,128,128]{2,0,1:T(8,128)S(1)} %bitcast.133, f32[128,128,128]{2,1,0:T(8,128)} %gather_fusion.2), kind=kOutput, calls=%fused_computation.146 | convolution fusion | flops 402653184 | bytes 10485760 | tf_op jit(solution)/shard_map/bij,sbj->sbi/dot_general | solution.py:75
  56.7 14.2 %fusion.53 = f32[128,16,128]{2,1,0:T(8,128)} fusion(f32[16,128,128]{2,0,1:T(8,128)S(1)} %bitcast.134, f32[128,128,128]{2,1,0:T(8,128)S(1)} %copy-done), kind=kOutput, calls=%fused_computation.147 | convolution fusion | flops 402653184 | bytes 10485760 | tf_op jit(solution)/shard_map/bij,sbj->sbi/dot_general | solution.py:75
  75.1 4.7 scatter_custom_fusion
  80.8 5.4 collective-permute-start.3
  95.2 128.8 %all-reduce.5.cloned.1.call-done = f32[256,256]{0,1:T(8,128)} async-done(((f32[256,256]{0,1:T(8,128)}), f32[256,256]{0,1:T(8,128)}) %all-reduce.5.cloned.1.call-update) | async-done | bytes 262160 | tf_op jit(solution)/shard_map/psum | solution.py:89
  226.1 11.7 %cholesky.50 = f32[128,128]{1,0:T(8,128)S(1)} custom-call(f32[128,128]{1,0:T(8,128)S(1)} %cholesky.118), custom_call_target="Cholesky" | custom-call | tf_op jit(solution)/shard_map/jit(cholesky)/cholesky | solution.py:90
  237.9 9.8 %custom-call.16 = f32[1,128,128]{1,2,0:T(8,128)S(1)} custom-call(f32[1,128,128]{2,1,0:T(8,128)S(1)} %get-tuple-element.55), custom_call_target="InvertDiagBlocksLowerTriangular" | custom-call | tf_op jit(solution)/shard_map/jit(cholesky)/cholesky | solution.py:90
  248.2 11.7 %cholesky.105 = f32[128,128]{1,0:T(8,128)S(1)} custom-call(f32[128,128]{1,0:T(8,128)S(1)} %convolution_subtract_fusion), custom_call_target="Cholesky" | custom-call | tf_op jit(solution)/shard_map/jit(cholesky)/cholesky | solution.py:90
  261.9 4.0 while.4
  265.9 19.7 %custom-call.20 = f32[2,128,128]{1,2,0:T(8,128)S(1)} custom-call(f32[2,128,128]{2,1,0:T(8,128)S(1)} %get-tuple-element.17), custom_call_target="InvertDiagBlocksLowerTriangular" | custom-call | tf_op jit(solution)/shard_map/jit(_cho_solve)/triangular_solve | solution.py:108
  293.3 4.0 collective-permute-done.7
  297.4 9.8 %collective-permute-start.8 = (f32[16,10,1,128]{3,0,2,1:T(8,128)S(1)}, f32[16,10,1,128]{3,0,2,1:T(8,128)S(1)}, u32[]{:S(2)}, u32[]{:S(2)}) collective-permute-start(f32[16,10,1,128]{3,0,2,1:T(8,128)S(1)} %get-tuple-element.44), channel_id=1, source_target_pairs={{0,1},{1,2},{2,3},{3,4},{4,5},{5,6},{6,7},{8,9},{9,10},{10,11},{11... | collective-permute-start | bytes 245768 | tf_op jit(solution)/shard_map/ppermute | solution.py:19
  309.1 15.4 %fusion.54 = f32[128,16,128]{2,1,0:T(8,128)S(1)} fusion(f32[16,128,128]{2,0,1:T(8,128)S(1)} %bitcast.124, f32[128,128,128]{2,1,0:T(8,128)} %gather_fusion.2), kind=kOutput, calls=%fused_computation.148 | convolution fusion | flops 402653184 | bytes 10485760 | tf_op jit(solution)/shard_map/bij,sbj->sbi/dot_general | solution.py:75
  326.3 77.1 %all-reduce.2 = (f32[16]{0:T(128)S(1)}, f32[16]{0:T(128)S(1)}) all-reduce(f32[16]{0:T(128)S(1)} %get-tuple-element.22, f32[16]{0:T(128)S(1)} %get-tuple-element.21), channel_id=1, replica_groups=mesh['row'=32,'col'=8] {'row','col'}, use_global_device_ids=true, to_apply=%region_12.14 | all-reduce | flops 32 | bytes 256 | tf_op jit(solution)/shard_map/psum | solution.py:58
  405.4 16.2 %divide_add_fusion = (f32[16,8,16,128]{3,0,2,1:T(8,128)}, f32[16,8,16]{0,2,1:T(8,128)S(1)}, f32[128,16,128]{2,1,0:T(8,128)S(1)}) fusion(f32[16,8,16,128]{3,0,2,1:T(8,128)S(1)} %get-tuple-element.38, f32[128]{0:T(128)S(1)} %add_multiply_fusion, f32[8,16,128]{2,1,0:T(8,128)S(1)} %broadcast_add_fusion, f32[16,128,128]{2,0,1:T(8,128)S(1)} %bitcast.132, ...), kind=kOutput, calls=%fused_computation.52 | convolution fusion | flops 404486144 | bytes 12657152 | tf_op jit(solution)/shard_map/bij,sbj->sbi/dot_general | solution.py:75
  432.7 4.4 collective-permute-done.12
  441.1 16.6 %fusion.55 = f32[128,16,128]{2,1,0:T(8,128)} fusion(f32[16,128,128]{2,0,1:T(8,128)} %bitcast.131, f32[128,128,128]{2,1,0:T(8,128)} %gather_fusion.2), kind=kOutput, calls=%fused_computation.149 | convolution fusion | flops 402653184 | bytes 10485760 | tf_op jit(solution)/shard_map/bij,sbj->sbi/dot_general | solution.py:75
  461.5 76.5 %psum.38 = f32[16]{0:T(128)S(1)} all-reduce(f32[16]{0:T(128)S(1)} %multiply_reduce_fusion.1), channel_id=1, replica_groups=mesh['row'=32,'col'=8] {'row','col'}, use_global_device_ids=true, to_apply=%region_18.20 | all-reduce | flops 16 | bytes 128 | tf_op jit(solution)/shard_map/psum | solution.py:58
  540.8 3.7 collective-permute-start.15
  550.2 4.5 collective-permute-start.17
  556.6 15.7 %fusion.56 = f32[128,16,128]{2,1,0:T(8,128)S(1)} fusion(f32[16,128,128]{2,0,1:T(8,128)S(1)} %bitcast.125, f32[128,128,128]{2,1,0:T(8,128)} %gather_fusion.2), kind=kOutput, calls=%fused_computation.150 | convolution fusion | flops 402653184 | bytes 10485760 | tf_op jit(solution)/shard_map/bij,sbj->sbi/dot_general | solution.py:75
  573.8 75.3 %psum.39 = f32[16]{0:T(128)S(1)} all-reduce(f32[16]{0:T(128)S(1)} %get-tuple-element.35), channel_id=1, replica_groups=mesh['row'=32,'col'=8] {'row','col'}, use_global_device_ids=true, to_apply=%region_20.22 | all-reduce | flops 16 | bytes 128 | tf_op jit(solution)/shard_map/psum | solution.py:129
  (167 shorter events, 89.9 us)
Async XLA Ops:
  7.2 27.4 %copy-start.2 = (f32[16,8,16,128]{3,2,1,0:T(8,128)S(1)}, f32[16,8,16,128]{3,2,1,0:T(8,128)}, u32[]{:S(2)}) copy-start(f32[16,8,16,128]{3,2,1,0:T(8,128)} %param.7) | copy-start | bytes 3145732
  7.2 216.8 %all-reduce.5.cloned.1.call-start = ((), (), s32[]{:S(2)}) async-start(), calls=%async_computation | async-start | bytes 524288 | tf_op jit(solution)/shard_map/psum | solution.py:89
  8.0 63.1 %collective-permute-start = (s32[16]{0:T(128)S(1)}, s32[16]{0:T(128)S(1)}, u32[]{:S(2)}, u32[]{:S(2)}) collective-permute-start(s32[16]{0:T(128)S(1)} %slice_bitcast_fusion.10), channel_id=1, source_target_pairs={{8,0},{16,8},{24,16},{32,24},{40,32},{48,40},{56,48},{64,56},{72,6... | collective-permute-start | bytes 200 | tf_op jit(solution)/shard_map/ppermute | solution.py:28
  13.0 58.8 %collective-permute-start.1 = (f32[256,16]{0,1:T(8,128)S(1)}, f32[256,16]{0,1:T(8,128)S(1)}, u32[]{:S(2)}, u32[]{:S(2)}) collective-permute-start(f32[256,16]{0,1:T(8,128)S(1)} %copy.56), channel_id=1, source_target_pairs={{0,8},{8,0},{16,24},{24,16},{32,40},{40,32},{48,56},{56,48},{64,72... | collective-permute-start | bytes 49160 | tf_op jit(solution)/shard_map/ppermute | solution.py:105
  71.8 8.9 %collective-permute-start.2 = (f32[256,16]{0,1:T(8,128)S(1)}, f32[256,16]{0,1:T(8,128)S(1)}, u32[]{:S(2)}, u32[]{:S(2)}) collective-permute-start(f32[256,16]{0,1:T(8,128)S(1)} %add.265), channel_id=1, source_target_pairs={{0,16},{8,24},{16,0},{24,8},{32,48},{40,56},{48,32},{56,40},{64,80... | collective-permute-start | bytes 49160 | tf_op jit(solution)/shard_map/ppermute | solution.py:105
  80.8 7.0 %collective-permute-start.3 = (f32[256,16]{0,1:T(8,128)S(1)}, f32[256,16]{0,1:T(8,128)S(1)}, u32[]{:S(2)}, u32[]{:S(2)}) collective-permute-start(f32[256,16]{0,1:T(8,128)S(1)} %add.266), channel_id=1, source_target_pairs={{0,32},{8,40},{16,48},{24,56},{32,0},{40,8},{48,16},{56,24},{64,96... | collective-permute-start | bytes 49160 | tf_op jit(solution)/shard_map/ppermute | solution.py:105
  87.8 3.3 collective-permute-start.4
  91.0 4.2 collective-permute-start.5
  289.6 3.7 collective-permute-start.6
  291.4 5.9 collective-permute-start.7
  297.4 27.1 %collective-permute-start.8 = (f32[16,10,1,128]{3,0,2,1:T(8,128)S(1)}, f32[16,10,1,128]{3,0,2,1:T(8,128)S(1)}, u32[]{:S(2)}, u32[]{:S(2)}) collective-permute-start(f32[16,10,1,128]{3,0,2,1:T(8,128)S(1)} %get-tuple-element.44), channel_id=1, source_target_pairs={{0,1},{1,2},{2,3},{3,4},{4,5},{5,6},{6,7},{8,9},{9,10},{10,11},{11... | collective-permute-start | bytes 245768 | tf_op jit(solution)/shard_map/ppermute | solution.py:19
  307.1 17.3 %collective-permute-start.9 = (f32[16,10,1,128]{3,0,2,1:T(8,128)S(1)}, f32[16,10,1,128]{3,0,2,1:T(8,128)S(1)}, u32[]{:S(2)}, u32[]{:S(2)}) collective-permute-start(f32[16,10,1,128]{3,0,2,1:T(8,128)S(1)} %get-tuple-element.45), channel_id=1, source_target_pairs={{1,0},{2,1},{3,2},{4,3},{5,4},{6,5},{7,6},{9,8},{10,9},{11,10},{12... | collective-permute-start | bytes 245768 | tf_op jit(solution)/shard_map/ppermute | solution.py:20
  421.6 116.5 %copy-start.3 = (f32[128,16,128]{2,1,0:T(8,128)}, f32[128,16,128]{2,1,0:T(8,128)S(1)}, u32[]{:S(2)}) copy-start(f32[128,16,128]{2,1,0:T(8,128)S(1)} %get-tuple-element.72) | copy-start | bytes 3145732
  424.5 33.2 %copy-start.5 = (f32[2,128,128]{1,2,0:T(8,128)S(1)}, f32[2,128,128]{1,2,0:T(8,128)}, u32[]{:S(2)}) copy-start(f32[2,128,128]{1,2,0:T(8,128)} %copy-done.4) | copy-start | bytes 393220
  424.5 2.7 collective-permute-start.10
  427.1 3.5 collective-permute-start.11
  430.6 6.5 collective-permute-start.12
  437.1 2.9 collective-permute-start.13
  440.0 17.7 %collective-permute-start.14 = (f32[256,16]{0,1:T(8,128)S(1)}, f32[256,16]{0,1:T(8,128)S(1)}, u32[]{:S(2)}, u32[]{:S(2)}) collective-permute-start(f32[256,16]{0,1:T(8,128)S(1)} %add.283), channel_id=1, source_target_pairs={{0,128},{8,136},{16,144},{24,152},{32,160},{40,168},{48,176},{56,1... | collective-permute-start | bytes 49160 | tf_op jit(solution)/shard_map/ppermute | solution.py:105
  540.8 108.3 %copy-start.8 = (f32[16]{0:T(128)S(1)}, f32[16]{0:T(128)}, u32[]{:S(2)}) copy-start(f32[16]{0:T(128)} %copy-done.7) | copy-start | bytes 196
  540.8 5.8 collective-permute-start.15
  544.5 5.7 collective-permute-start.16
  550.2 22.1 %collective-permute-start.17 = (f32[16,10,1,128]{3,0,2,1:T(8,128)S(1)}, f32[16,10,1,128]{3,0,2,1:T(8,128)S(1)}, u32[]{:S(2)}, u32[]{:S(2)}) collective-permute-start(f32[16,10,1,128]{3,0,2,1:T(8,128)S(1)} %get-tuple-element.42), channel_id=1, source_target_pairs={{0,1},{1,2},{2,3},{3,4},{4,5},{5,6},{6,7},{8,9},{9,10},{10,11},{11... | collective-permute-start | bytes 245768 | tf_op jit(solution)/shard_map/ppermute | solution.py:19
  554.7 17.6 %collective-permute-start.18 = (f32[16,10,1,128]{3,0,2,1:T(8,128)S(1)}, f32[16,10,1,128]{3,0,2,1:T(8,128)S(1)}, u32[]{:S(2)}, u32[]{:S(2)}) collective-permute-start(f32[16,10,1,128]{3,0,2,1:T(8,128)S(1)} %get-tuple-element.43), channel_id=1, source_target_pairs={{1,0},{2,1},{3,2},{4,3},{5,4},{6,5},{7,6},{9,8},{10,9},{11,10},{12... | collective-permute-start | bytes 245768 | tf_op jit(solution)/shard_map/ppermute | solution.py:20
  (7 other events, 71.4 us)
Sparse Core Ops, SparseCore 0:
  80.9 143.1 all-reduce.4
